TPU v7x, 512 devices: a whole 4x4x16 slice. The times are simulated.
512 devices in a mesh: ctx: 64 (over x, z), fsdp: 8 (over y, core).
Axes of the slice: x: 4, y: 4, z: 16, core: 2. Of those that a mesh axis runs over, the one named last changes fastest.
Arguments:
- tokens: bfloat16 [8, 8192, 4096], P('fsdp', 'ctx'), may hold values from -6 to 6
- queries: bfloat16 [8, 8192, 512], P('fsdp', 'ctx'), may hold values from -6 to 6
- flags: int32 [8, 8192], P('fsdp', 'ctx'), may hold values from 0 to 1, as said below
- w_key: bfloat16 [4096, 512], P(('ctx', 'fsdp')), may hold values from -0.09375 to 0.09375
- w_value: bfloat16 [4096, 512], P(('ctx', 'fsdp')), may hold values from -0.09375 to 0.09375
- norm_gain: float32 [512], replicated, may hold values from 0.25 to 1.75
Outputs:
- attended: bfloat16 [8, 8192, 512], P('fsdp', 'ctx')
Inputs may be any that keep to these rules, and one draw needn't show every extreme that they name: `flags`: in each sequence a document starts at token 0 and at every token k * 2048 + 2048 // 2; other tokens start one at random, never before token 3072 and never at the first token of a block. No document is longer than 2048 tokens.
All inputs are finite; a program needn't handle non-finite values.
Results may differ from a plain program's by a relative error of at most 0.0053.
Values may be sent and summed in bfloat16 or wider, within the bound.
A program may use at most 64 MiB of HBM per device.

v0:
```python
import jax
import jax.numpy as jnp
from jax import lax
from jax.sharding import PartitionSpec as P

HEAD = 128


def entering(array, axis, join, neutral):
    place = lax.axis_index(axis)
    gathered = jax.tree.map(
        lambda a, kind: lax.all_gather(a.astype(kind), axis), array, (jnp.bfloat16, jnp.bfloat16)
    )
    state = jax.tree.map(lambda a, e: jnp.zeros_like(a) + jnp.asarray(e, a.dtype), array, neutral)

    def one(lap, state):
        return join(
            state,
            jax.tree.map(
                lambda a, own: lax.dynamic_index_in_dim(a, lap, 0, False).astype(own.dtype),
                gathered,
                array,
            ),
        )

    return lax.fori_loop(0, place, one, state)


def feature(u):
    return jax.nn.elu(u) + 1.0


def combine(earlier, later):
    keep = 1.0 - later[0][0]
    return (jnp.maximum(earlier[0], later[0]), later[1] + keep * earlier[1])


def on_device(tokens, queries, flags, w_key, w_value, norm_gain):
    rows = tokens[0]
    count = rows.shape[0]
    width = w_key.shape[1]
    heads = width // HEAD
    full_panels = (
        lax.all_gather(w_key, ("ctx", "fsdp"), axis=0, tiled=True),
        lax.all_gather(w_value, ("ctx", "fsdp"), axis=0, tiled=True),
    )
    proj_key = jnp.dot(rows, full_panels[0], preferred_element_type=jnp.float32)
    proj_value = jnp.dot(rows, full_panels[1], preferred_element_type=jnp.float32)
    key = feature(proj_key).astype(jnp.bfloat16).reshape(count, heads, HEAD)
    value = proj_value.astype(jnp.bfloat16).reshape(count, heads, HEAD)
    query = feature(queries[0].astype(jnp.float32)).astype(jnp.bfloat16).reshape(count, heads, HEAD)
    seg = jnp.cumsum(flags[0])
    last = seg[count - 1]
    reset = (last > 0).astype(jnp.float32).reshape(1)
    tail = (seg == last).astype(jnp.bfloat16)
    local_state = jnp.einsum(
        "the,thf->hef", key * tail[:, None, None], value, preferred_element_type=jnp.float32
    )
    identity = (jnp.zeros((1,), jnp.float32), jnp.zeros_like(local_state))
    carried = entering((reset, local_state), "ctx", combine, identity)
    carried_b = carried[1].astype(jnp.bfloat16)
    places = jnp.arange(count, dtype=jnp.int32)
    allowed = (places[None, :] <= places[:, None]) & (seg[None, :] == seg[:, None])
    scores = jnp.einsum("the,she->hts", query, key, preferred_element_type=jnp.float32)
    scores = jnp.where(allowed[None, :, :], scores, 0.0).astype(jnp.bfloat16)
    inside = jnp.einsum("hts,shf->thf", scores, value, preferred_element_type=jnp.float32)
    first = (seg == 0).astype(jnp.float32)
    carried_term = (
        jnp.einsum("the,hef->thf", query, carried_b, preferred_element_type=jnp.float32)
        * first[:, None, None]
    )
    mixed = carried_term + inside
    scale = lax.rsqrt(jnp.mean(mixed * mixed, axis=-1, keepdims=True) + 1e-06)
    attended = (mixed * scale * norm_gain.reshape(heads, HEAD)).astype(jnp.bfloat16)
    return attended.reshape(1, count, width)


def solution(mesh):
    in_specs = (
        P("fsdp", "ctx", None),
        P("fsdp", "ctx", None),
        P("fsdp", "ctx"),
        P(("ctx", "fsdp"), None),
        P(("ctx", "fsdp"), None),
        P(),
    )
    out_specs = P("fsdp", "ctx", None)
    return jax.shard_map(
        on_device, mesh=mesh, in_specs=in_specs, out_specs=out_specs, check_vma=False
    )
```

profile of v0, /device:TPU:486, one launch (start us, length us, event | category | flops | bytes accessed | tf_op | source)
XLA Modules:
  0.0 710.5 jit_solution(16022774016434404635)
XLA Ops:
  10.1 196.2 %all-gather.7.cloned.1.call-done = bf16[4096,512]{1,0:T(8,128)(2,1)} async-done(((bf16[8,512]{1,0:T(8,128)(2,1)}), bf16[4096,512]{1,0:T(8,128)(2,1)}) %all-gather.7.cloned.1.call-update) | async-done | bytes 4194320 | tf_op jit(solution)/shard_map/all_gather | solution.py:45
  206.4 2.9 convolution_convert_fusion
  209.4 195.0 %all-gather.5.cloned.1.call-done = bf16[4096,512]{1,0:T(8,128)(2,1)} async-done(((bf16[8,512]{1,0:T(8,128)(2,1)}), bf16[4096,512]{1,0:T(8,128)(2,1)}) %all-gather.5.cloned.1.call-update) | async-done | bytes 4194320 | tf_op jit(solution)/shard_map/all_gather | solution.py:44
  404.4 3.0 fusion.11
  411.1 138.5 %all-reduce = bf16[64]{0:T(256)(128)(2,1)S(1)} all-reduce(bf16[64]{0:T(256)(128)(2,1)S(1)} %dynamic-update-slice), channel_id=1, replica_groups=mesh['ctx'=64,'fsdp'=8] {'ctx'}, use_global_device_ids=true, to_apply=%add | all-reduce | flops 64 | bytes 256
  549.6 10.8 %all-gather.9.cloned.1.call-done = bf16[256,128,128]{2,1,0:T(8,128)(2,1)} async-done(((bf16[4,128,128]{2,1,0:T(8,128)(2,1)}), bf16[256,128,128]{2,1,0:T(8,128)(2,1)}) %all-gather.9.cloned.1.call-update) | async-done | bytes 8388624 | tf_op jit(solution)/shard_map/all_gather | solution.py:12
  560.4 142.0 %while.12 = (s32[]{:T(128)}, f32[4,128,128]{2,1,0:T(8,128)S(1)}, s32[]{:T(128)}, bf16[64,4,128,128]{3,2,1,0:T(8,128)(2,1)}, bf16[64,1]{0,1:T(2,128)(2,1)S(1)}, /*index=5*/s32[]{:T(128)}, s32[]{:T(128)}, s32[]{:T(128)}) while((s32[]{:T(128)}, f32[4,128,128]{2,1,0:T(8,128)S(1)}, s32[]{:T(128)}, bf16[64,4,128,128]{3,2,1,0:T(8,128)(2,1)}, ...), condition=%wide.region_2.3_spmd, body=%wide.region_1.2_spmd.sunk | while | flops 196614 | bytes 655505 | solution.py:26
  561.1 1.6 convert_add_fusion.2
  563.3 1.6 convert_add_fusion.2
  565.6 1.6 convert_add_fusion.2
  567.8 1.6 convert_add_fusion.2
  570.1 1.6 convert_add_fusion.2
  572.3 1.6 convert_add_fusion.2
  574.6 1.6 convert_add_fusion.2
  576.8 1.6 convert_add_fusion.2
  579.1 1.6 convert_add_fusion.2
  581.3 1.6 convert_add_fusion.2
  583.6 1.6 convert_add_fusion.2
  585.8 1.6 convert_add_fusion.2
  588.1 1.6 convert_add_fusion.2
  590.3 1.6 convert_add_fusion.2
  592.6 1.6 convert_add_fusion.2
  594.9 1.6 convert_add_fusion.2
  597.1 1.6 convert_add_fusion.2
  599.4 1.6 convert_add_fusion.2
  601.6 1.6 convert_add_fusion.2
  603.9 1.6 convert_add_fusion.2
  606.1 1.6 convert_add_fusion.2
  608.4 1.6 convert_add_fusion.2
  610.6 1.6 convert_add_fusion.2
  612.9 1.6 convert_add_fusion.2
  615.1 1.6 convert_add_fusion.2
  617.4 1.6 convert_add_fusion.2
  619.6 1.6 convert_add_fusion.2
  621.9 1.6 convert_add_fusion.2
  624.1 1.6 convert_add_fusion.2
  626.4 1.6 convert_add_fusion.2
  628.6 1.6 convert_add_fusion.2
  630.9 1.6 convert_add_fusion.2
  633.2 1.6 convert_add_fusion.2
  635.4 1.6 convert_add_fusion.2
  637.7 1.6 convert_add_fusion.2
  639.9 1.6 convert_add_fusion.2
  642.2 1.6 convert_add_fusion.2
  644.4 1.6 convert_add_fusion.2
  646.7 1.6 convert_add_fusion.2
  648.9 1.6 convert_add_fusion.2
  651.2 1.6 convert_add_fusion.2
  653.4 1.6 convert_add_fusion.2
  655.7 1.6 convert_add_fusion.2
  657.9 1.6 convert_add_fusion.2
  660.2 1.6 convert_add_fusion.2
  662.4 1.6 convert_add_fusion.2
  664.7 1.6 convert_add_fusion.2
  667.0 1.6 convert_add_fusion.2
  669.2 1.6 convert_add_fusion.2
  671.5 1.6 convert_add_fusion.2
  673.7 1.6 convert_add_fusion.2
  676.0 1.6 convert_add_fusion.2
  678.2 1.6 convert_add_fusion.2
  680.5 1.6 convert_add_fusion.2
  682.7 1.6 convert_add_fusion.2
  696.2 1.6 convert_add_fusion.2
  698.5 1.6 convert_add_fusion.2
  (100 shorter events, 55.4 us)
Async XLA Ops:
  6.5 199.8 %copy-start = (bf16[1,128,4096]{2,1,0:T(8,128)(2,1)S(1)}, bf16[1,128,4096]{2,1,0:T(8,128)(2,1)}, u32[]{:S(2)}) copy-start(bf16[1,128,4096]{2,1,0:T(8,128)(2,1)} %param.8) | copy-start | bytes 3145732
  6.5 199.8 %all-gather.7.cloned.1.call-start = ((), (), s32[]{:S(2)}) async-start(), calls=%async_computation.1 | async-start | bytes 4202496 | tf_op jit(solution)/shard_map/all_gather | solution.py:45
  7.3 397.1 %all-gather.5.cloned.1.call-start = ((), (), s32[]{:S(2)}) async-start(), calls=%async_computation | async-start | bytes 4202496 | tf_op jit(solution)/shard_map/all_gather | solution.py:44
  8.0 552.4 %all-gather.9.cloned.1.call-start = ((), (), s32[]{:S(2)}) async-start(), calls=%async_computation.2 | async-start | bytes 8519680 | tf_op jit(solution)/shard_map/all_gather | solution.py:12
  209.3 199.7 %copy-start.1 = (bf16[1,128,512]{2,1,0:T(8,128)(2,1)S(1)}, bf16[1,128,512]{2,1,0:T(8,128)(2,1)}, u32[]{:S(2)}) copy-start(bf16[1,128,512]{2,1,0:T(8,128)(2,1)} %param.9) | copy-start | bytes 393220
  407.4 295.7 %copy-start.2 = (f32[512]{0:T(512)S(1)}, f32[512]{0:T(512)}, u32[]{:S(2)}) copy-start(f32[512]{0:T(512)} %param.13) | copy-start | bytes 6148
Sparse Core Ops, SparseCore 0:
  11.9 194.3 all-gather.6
  210.9 193.3 all-gather.4
  408.5 151.8 all-gather.8
where the time goes:
time: 712 us; the launch traced here: 711 us
  waiting for transfers between devices  403 us (57%)
  other arithmetic  142 us (20%)
  blocking collectives  138 us (19%)
  between operations  13.8 us (2%)
  matrix products  7.42 us (1%)
    all_gather x1, waiting for transfers between devices, on_device(): lax.all_gather(w_value, ('ctx', 'fsdp'), axis=0, tiled=True)  196 us
    all_gather x1, waiting for transfers between devices, on_device(): lax.all_gather(w_key, ('ctx', 'fsdp'), axis=0, tiled=True)  195 us
    unnamed x1, blocking collectives  138 us
    add x63, other arithmetic, combine(): return (jnp.maximum(earlier[0], later[0]), later[1] + keep * earlier[1])  104 us
    sub x63, other arithmetic, combine(): keep = 1.0 - later[0][0]  37.1 us
  transfers between devices with their start and end apart: 3, of which 3 were waited for; matrix products, arithmetic and copies ran while one was open for 1% of the time, Pallas kernels for 0%

commit v1 on v0

v1 whole, which is shorter than its diff:
```python
import functools

import jax
import jax.numpy as jnp
from jax import lax
from jax.experimental import pallas as pl
from jax.experimental.pallas import tpu as pltpu
from jax.sharding import PartitionSpec as P

HEAD = 128
MESH = pl.DeviceIdType.MESH
NX, NY, NZ = 4, 4, 16
GROUP = 16
F32, BF16 = jnp.float32, jnp.bfloat16


def device(x, z, y, c):
    return (x * NZ + z, y * 2 + c)


def phi(u):
    return jnp.where(u > 0, u + 1.0, jnp.exp(jnp.minimum(u, 0.0)))


def segments(marks):
    n = marks.shape[1]
    t = lax.broadcasted_iota(jnp.int32, (n, n), 0)
    s = lax.broadcasted_iota(jnp.int32, (n, n), 1)
    wide = jnp.broadcast_to(marks, (n, n)).astype(F32)
    column = jnp.sum(jnp.where(s <= t, wide, 0.0), axis=1, keepdims=True)
    upright = jnp.sum(jnp.where(s == t, wide, 0.0), axis=1, keepdims=True)
    row = jnp.sum(jnp.where(t <= s, jnp.broadcast_to(upright, (n, n)), 0.0), axis=0, keepdims=True)
    last = jnp.sum(marks.astype(F32), axis=1, keepdims=True)
    return column, row, last


def kernel(
    tok, qry, flg, wk, wv, gain, out,
    T, Q, F, WB, W, acc, KV, KB, KR, ST, SR, CS, CR, MIX,
    loc, pair_s, pair_r, z_s, z_r, two_s, two_r, three_s, three_r, k_s, k_r, s1_s, s1_r, s2_s, s2_r,
):
    ctx, fsdp = lax.axis_index("ctx"), lax.axis_index("fsdp")
    x, z = ctx // NZ, lax.rem(ctx, NZ)
    y, c = fsdp // 2, lax.rem(fsdp, 2)
    other = 1 - c
    sibling = device(x, z, y, other)

    loads = [
        pltpu.make_async_copy(wk, WB.at[c, 0], loc.at[0]),
        pltpu.make_async_copy(wv, WB.at[c, 1], loc.at[1]),
        pltpu.make_async_copy(flg, F.at[c], loc.at[2]),
        pltpu.make_async_copy(tok, T.at[c], loc.at[3]),
        pltpu.make_async_copy(qry, Q, loc.at[4]),
    ]
    for load in loads:
        load.start()

    barrier = pltpu.get_barrier_semaphore()

    def greet(to):
        pl.semaphore_signal(barrier, inc=1, device_id=to, device_id_type=MESH)

    def greet_z(d, carry):
        greet(device(x, lax.rem(z + d, NZ), y, c))
        return carry

    lax.fori_loop(1, NZ, greet_z, 0)
    for d in range(1, 4):
        greet(device(lax.rem(x + d, NX), z, y, c))
        greet(device(x, z, lax.rem(y + d, NY), c))
    greet(sibling)
    for load in loads[:3]:
        load.wait()
    pl.semaphore_wait(barrier, 22)

    def send(src, dst, ss, rs, to):
        return pltpu.make_async_remote_copy(
            src_ref=src, dst_ref=dst, send_sem=ss, recv_sem=rs, device_id=to, device_id_type=MESH
        )

    swap_w = send(WB.at[c], WB.at[c], pair_s.at[0], pair_r.at[0], sibling)
    swap_f = send(F.at[c], F.at[c], pair_s.at[1], pair_r.at[1], sibling)
    swap_w.start()
    swap_f.start()
    swap_w.wait()
    both = jnp.concatenate([WB[0].astype(F32), WB[1].astype(F32)], axis=1)
    low, high = both[:, :, : 2 * HEAD], both[:, :, 2 * HEAD :]
    mine = jnp.where(c == 0, low, high).astype(BF16)
    for h in range(2):
        cut = slice(h * HEAD, (h + 1) * HEAD)
        W[h, x, z, y] = jnp.concatenate([mine[0, :, cut], mine[1, :, cut]], axis=1)

    def z_copy(d):
        piece = W.at[:, x, z, y]
        return send(piece, piece, z_s.at[d], z_r.at[d], device(x, lax.rem(z + d, NZ), y, c))

    def z_start(d, carry):
        z_copy(d).start()
        return carry

    def z_wait(d, carry):
        z_copy(d).wait()
        return carry

    lax.fori_loop(1, NZ, z_start, 0)
    loads[3].wait()
    swap_t = send(T.at[c], T.at[c], pair_s.at[2], pair_r.at[2], sibling)
    swap_t.start()
    swap_f.wait()
    lax.fori_loop(1, NZ, z_wait, 0)

    def two(d):
        a, b = W.at[0, x, :, y], W.at[1, x, :, y]
        return (
            send(a, a, two_s.at[0, d], two_r.at[0, d], device(x, z, lax.rem(y + d, NY), c)),
            send(b, b, two_s.at[1, d], two_r.at[1, d], device(lax.rem(x + d, NX), z, y, c)),
        )

    seconds = [two(d) for d in (1, 3, 2)]
    for pair in seconds:
        for copy in pair:
            copy.start()

    column, row, last = [], [], []
    for s in range(2):
        a, b, l = segments(F[s])
        column.append(a)
        row.append(b)
        last.append(l)
    for s in range(2):
        keep = jnp.where(last[s] > 0, 0.0, 1.0)
        KB[s] = jnp.broadcast_to(keep, (8, HEAD))
    for pair in seconds:
        for copy in pair:
            copy.wait()

    def three_a(d):
        a = W.at[0, x]
        return send(a, a, three_s.at[0, d], three_r.at[0, d], device(lax.rem(x + d, NX), z, y, c))

    def three_b(d, part):
        b = W.at[1, part, :, y]
        return send(b, b, three_s.at[1 + part, d], three_r.at[1 + part, d], device(x, z, lax.rem(y + d, NY), c))

    for d in (1, 3, 2):
        three_a(d).start()
    for part in range(NX):
        for d in (1, 3, 2):
            three_b(d, part).start()

    swap_t.wait()
    depth = NZ * NY * 16

    def project(h, part):
        cols = pl.ds(pl.multiple_of(part * depth, depth), depth)
        rows = jnp.concatenate([T[0, :, cols], T[1, :, cols]], axis=0)
        return jnp.dot(rows, W[h, part].reshape(depth, 2 * HEAD), preferred_element_type=F32)

    acc[0] = project(0, x)
    for d in (1, 3, 2):
        three_a(d).wait()
        acc[0] += project(0, lax.rem(x - d + NX, NX))
    acc[1] = jnp.zeros_like(acc[1])
    for part in range(NX):
        for d in (1, 3, 2):
            three_b(d, part).wait()
        acc[1] += project(1, part)

    place = lax.rem(z + NZ // 2, GROUP)
    base = lax.rem(x + NX - jnp.where(place < GROUP // 2, 0, 1), NX)

    def member(p, core):
        return device(
            lax.rem(base + p // (GROUP // 2), NX), lax.rem(p + NZ // 2, NZ), y, core
        )

    def keep_copy(d):
        return send(KB, KR.at[place], k_s.at[d], k_r.at[d], member(lax.rem(place + d, GROUP), c))

    def one_copy(d):
        p = lax.rem(place + d, GROUP)
        return send(ST.at[p], SR.at[place], s1_s.at[d], s1_r.at[d], member(p, c))

    def keep_start(d, carry):
        keep_copy(d).start()
        return carry

    def one_start(d, carry):
        one_copy(d).start()
        return carry

    def one_wait(d, carry):
        one_copy(d).wait()
        keep_copy(d).wait()
        return carry

    lax.fori_loop(1, GROUP, keep_start, 0)
    KR[place] = KB[...]

    for s in range(2):
        tail = (column[s] == last[s]).astype(F32)
        for h in range(2):
            part = acc[h, s * HEAD : (s + 1) * HEAD, :]
            key = phi(part[:, :HEAD]).astype(BF16)
            value = part[:, HEAD:].astype(BF16)
            KV[s, 2 * c + h, 0] = key
            KV[s, 2 * c + h, 1] = value
            masked = (key.astype(F32) * tail).astype(BF16)
            state = lax.dot_general(masked, value, (((0,), (0,)), ((), ())), preferred_element_type=F32)
            slot = (s * 2 + h) * 4
            ST[slot : slot + 4] = state.astype(BF16).reshape(4, HEAD // 4, HEAD)
    lax.fori_loop(1, GROUP, one_start, 0)
    SR[place] = ST[place]
    given = KV.at[other, pl.ds(2 * c, 2)]
    swap_kv = send(given, given, pair_s.at[3], pair_r.at[3], sibling)
    swap_kv.start()

    loads[4].wait()
    my_column = jnp.where(c == 0, column[0], column[1])
    my_row = jnp.where(c == 0, row[0], row[1])
    t = lax.broadcasted_iota(jnp.int32, (HEAD, HEAD), 0)
    u = lax.broadcasted_iota(jnp.int32, (HEAD, HEAD), 1)
    allowed = (u <= t) & (my_column == my_row)
    Q[...] = phi(Q[...].astype(F32)).astype(BF16)
    swap_kv.wait()
    for h in range(4):
        query = Q[:, h * HEAD : (h + 1) * HEAD]
        key, value = KV[c, h, 0], KV[c, h, 1]
        scores = lax.dot_general(query, key, (((1,), (1,)), ((), ())), preferred_element_type=F32)
        scores = jnp.where(allowed, scores, 0.0).astype(BF16)
        MIX[h] = jnp.dot(scores, value, preferred_element_type=F32)

    lax.fori_loop(1, GROUP, one_wait, 0)
    seq = place // (GROUP // 2)

    def prefix(b, carried):
        CS[b] = carried.astype(BF16)
        return KR[b, seq][0:1, :] * carried + SR[b].astype(F32)

    lax.fori_loop(0, GROUP, prefix, jnp.zeros((HEAD // 4, HEAD), F32))

    mine_at = lax.rem(place, GROUP // 2)
    target = CR.at[2 * c + mine_at // 4, lax.rem(mine_at, 4)]
    index = c * 8 + mine_at

    def back_copy(d):
        p = lax.rem(place + d, GROUP)
        return send(CS.at[p], target, s2_s.at[d], s2_r.at[index], member(p, seq))

    def back_start(d, carry):
        back_copy(d).start()
        return carry

    def back_wait(d, carry):
        back_copy(d).wait_send()
        return carry

    own = pltpu.make_async_copy(CS.at[place], target, s2_r.at[index])

    @pl.when(seq == c)
    def _():
        own.start()

    @pl.when(seq != c)
    def _():
        back_copy(0).start()

    lax.fori_loop(1, GROUP, back_start, 0)

    def arrive(i, carry):
        send(CS.at[0], CR.at[i // 4, lax.rem(i, 4)], s2_s.at[0], s2_r.at[i], sibling).wait_recv()
        return carry

    lax.fori_loop(0, GROUP, arrive, 0)
    first = (my_column == 0).astype(F32)
    for h in range(4):
        query = Q[:, h * HEAD : (h + 1) * HEAD]
        state = CR[h].reshape(HEAD, HEAD)
        mixed = MIX[h] + first * jnp.dot(query, state, preferred_element_type=F32)
        scale = lax.rsqrt(jnp.mean(mixed * mixed, axis=-1, keepdims=True) + 1e-06)
        cut = slice(h * HEAD, (h + 1) * HEAD)
        out[:, cut] = (mixed * scale * gain[:, cut]).astype(BF16)

    @pl.when(seq != c)
    def _():
        back_copy(0).wait_send()

    lax.fori_loop(1, GROUP, back_wait, 0)


def on_device(tokens, queries, flags, w_key, w_value, norm_gain):
    count, width = queries.shape[1:]
    dma = pltpu.SemaphoreType.DMA
    any_spec = pl.BlockSpec(memory_space=pl.ANY)
    vmem_spec = pl.BlockSpec(memory_space=pltpu.VMEM)
    attended = pl.pallas_call(
        kernel,
        out_shape=jax.ShapeDtypeStruct((count, width), BF16),
        in_specs=[any_spec, any_spec, any_spec, any_spec, any_spec, vmem_spec],
        out_specs=vmem_spec,
        scratch_shapes=[
            pltpu.VMEM((2, count, tokens.shape[2]), BF16),
            pltpu.VMEM((count, width), BF16),
            pltpu.VMEM((2, 1, count), jnp.int32),
            pltpu.VMEM((2, 2, 8, width), BF16),
            pltpu.VMEM((2, NX, NZ, NY, 16, 2 * HEAD), BF16),
            pltpu.VMEM((2, 2 * count, 2 * HEAD), F32),
            pltpu.VMEM((2, 4, 2, count, HEAD), BF16),
            pltpu.VMEM((2, 8, HEAD), F32),
            pltpu.VMEM((GROUP, 2, 8, HEAD), F32),
            pltpu.VMEM((GROUP, HEAD // 4, HEAD), BF16),
            pltpu.VMEM((GROUP, HEAD // 4, HEAD), BF16),
            pltpu.VMEM((GROUP, HEAD // 4, HEAD), BF16),
            pltpu.VMEM((4, 4, HEAD // 4, HEAD), BF16),
            pltpu.VMEM((4, count, HEAD), F32),
            dma((5,)),
            dma((4,)),
            dma((4,)),
            dma((NZ,)),
            dma((NZ,)),
            dma((2, 4)),
            dma((2, 4)),
            dma((5, 4)),
            dma((5, 4)),
            dma((GROUP,)),
            dma((GROUP,)),
            dma((GROUP,)),
            dma((GROUP,)),
            dma((GROUP,)),
            dma((GROUP,)),
        ],
        compiler_params=pltpu.CompilerParams(
            collective_id=0, has_side_effects=True, vmem_limit_bytes=40 << 20
        ),
        name="attention",
    )(tokens[0], queries[0], flags, w_key, w_value, norm_gain.reshape(1, width))
    return attended.reshape(1, count, width)


def solution(mesh):
    in_specs = (
        P("fsdp", "ctx", None),
        P("fsdp", "ctx", None),
        P("fsdp", "ctx"),
        P(("ctx", "fsdp"), None),
        P(("ctx", "fsdp"), None),
        P(),
    )
    out_specs = P("fsdp", "ctx", None)
    return jax.shard_map(
        on_device, mesh=mesh, in_specs=in_specs, out_specs=out_specs, check_vma=False
    )
```

time: 712 us -> 97.9 us (0.14)
  the two profiles are of different devices: /device:TPU:486 before, /device:TPU:24 now
where the time goes in v1:
time: 97.9 us; the launch traced here: 96.9 us
  Pallas kernels  92 us (94%)
  local copies, waits for them, and re-layouts  4.86 us (5%)
    pallas_call x1, Pallas kernels, on_device(): pl.pallas_call(kernel, out_shape=jax.ShapeDtypeStruct((count, width), BF1...  92 us
    unnamed x13, local copies, waits for them, and re-layouts  4.86 us

profile of v1, /device:TPU:24, one launch (start us, length us, event | category | flops | bytes accessed | tf_op | source)
XLA Modules:
  0.0 96.9 jit_solution(4027695543294042322)
XLA Ops:
  0.0 0.0 copy-start.4
  0.0 0.0 copy-start.5
  0.0 0.7 copy-done.4
  0.7 0.0 copy-done.5
  0.7 0.0 copy-start
  0.7 1.2 %copy-done = bf16[1,128,4096]{2,1,0:T(8,128)(2,1)S(1)} copy-done((bf16[1,128,4096]{2,1,0:T(8,128)(2,1)S(1)}, bf16[1,128,4096]{2,1,0:T(8,128)(2,1)}, u32[]{:S(2)}) %copy-start) | copy-done | bytes 1048600
  1.9 0.0 copy-start.1
  1.9 0.9 copy-done.1
  2.8 0.0 copy-start.2
  2.8 0.7 copy-done.2
  3.5 0.0 copy-start.3
  3.5 0.7 copy-done.3
  4.2 92.0 %attention.1 = bf16[128,512]{1,0:T(8,128)(2,1)S(1)} custom-call(bf16[128,4096]{1,0:T(8,128)(2,1)S(1)} %bitcast.4, bf16[128,512]{1,0:T(8,128)(2,1)S(1)} %bitcast.6, s32[1,128]{1,0:T(1,128)S(1)} %copy-done.5, bf16[8,512]{1,0:T(8,128)(2,1)S(1)} %copy-done.2, bf16[8,512]{1,0:T(8,128)(2,1)S(1)} %copy-done.3, f32[1,512]{1,0:T(1,128)S(1)} %bitcast.7), custom_call_target="tpu_custom_call" | custom-call | tf_op jit(solution)/shard_map/attention/pallas_call | solution.py:296
  96.2 0.7 copy.8
Async XLA Ops:
  0.0 0.7 copy-start.4
  0.0 0.7 copy-start.5
  0.7 1.2 %copy-start = (bf16[1,128,4096]{2,1,0:T(8,128)(2,1)S(1)}, bf16[1,128,4096]{2,1,0:T(8,128)(2,1)}, u32[]{:S(2)}) copy-start(bf16[1,128,4096]{2,1,0:T(8,128)(2,1)} %param.6) | copy-start | bytes 3145732
  1.9 0.9 copy-start.1
  2.8 0.7 copy-start.2
  3.5 0.7 copy-start.3

commit v2 on v1

v2 whole, which is shorter than its diff:
```python
import functools

import jax
import jax.numpy as jnp
from jax import lax
from jax.experimental import pallas as pl
from jax.experimental.pallas import tpu as pltpu
from jax.sharding import PartitionSpec as P

HEAD = 128
MESH = pl.DeviceIdType.MESH
NX, NY, NZ = 4, 4, 16
GROUP = 16
F32, BF16 = jnp.float32, jnp.bfloat16


def device(x, z, y, c):
    return (x * NZ + z, y * 2 + c)


def phi(u):
    return jnp.where(u > 0, u + 1.0, jnp.exp(jnp.minimum(u, 0.0)))


def segments(marks):
    n = marks.shape[1]
    t = lax.broadcasted_iota(jnp.int32, (n, n), 0)
    s = lax.broadcasted_iota(jnp.int32, (n, n), 1)
    wide = jnp.broadcast_to(marks, (n, n)).astype(F32)
    column = jnp.sum(jnp.where(s <= t, wide, 0.0), axis=1, keepdims=True)
    upright = jnp.sum(jnp.where(s == t, wide, 0.0), axis=1, keepdims=True)
    row = jnp.sum(jnp.where(t <= s, jnp.broadcast_to(upright, (n, n)), 0.0), axis=0, keepdims=True)
    last = jnp.sum(marks.astype(F32), axis=1, keepdims=True)
    return column, row, last


def kernel(
    tok, qry, flg, wk, wv, gain, out,
    T, Q, F, G, WB, W, acc, KV, KG, ST, SR, CS, CR, MIX,
    loc, pair_s, pair_r, z_s, z_r, k_s, k_r, two_s, two_r, three_s, three_r, s1_s, s1_r, s2_s, s2_r,
):
    ctx, fsdp = lax.axis_index("ctx"), lax.axis_index("fsdp")
    x, z = ctx // NZ, lax.rem(ctx, NZ)
    y, c = fsdp // 2, lax.rem(fsdp, 2)
    quad, low = z // 4, lax.rem(z, 4)
    other = 1 - c
    sibling = device(x, z, y, other)

    def at_x(d):
        return device(lax.rem(x + d, NX), z, y, c)

    def at_y(d):
        return device(x, z, lax.rem(y + d, NY), c)

    def at_z(d):
        return device(x, lax.rem(z + d, NZ), y, c)

    def in_quad(d):
        return device(x, quad * 4 + lax.rem(low + d, 4), y, c)

    loads = [
        pltpu.make_async_copy(wk, WB.at[c, 0], loc.at[0]),
        pltpu.make_async_copy(wv, WB.at[c, 1], loc.at[1]),
        pltpu.make_async_copy(flg, F.at[c], loc.at[2]),
        pltpu.make_async_copy(tok, T.at[c], loc.at[3]),
        pltpu.make_async_copy(qry, Q, loc.at[4]),
        pltpu.make_async_copy(gain, G, loc.at[5]),
    ]
    for load in loads:
        load.start()

    barrier = pltpu.get_barrier_semaphore()
    greeted = [sibling, at_z(4), at_z(12)]
    for d in range(1, 4):
        greeted += [at_x(d), at_y(d), in_quad(d)]
    for to in greeted:
        pl.semaphore_signal(barrier, inc=1, device_id=to, device_id_type=MESH)
    for load in loads[:3]:
        load.wait()
    pl.semaphore_wait(barrier, len(greeted))

    started = []

    def send(src, dst, ss, rs, to):
        return pltpu.make_async_remote_copy(
            src_ref=src, dst_ref=dst, send_sem=ss, recv_sem=rs, device_id=to, device_id_type=MESH
        )

    def same(ref, ss, rs, to):
        return send(ref, ref, ss, rs, to)

    def start(copies):
        for copy in copies:
            copy.start()
            started.append(copy)

    def arrive(copies):
        for copy in copies:
            copy.wait_recv()

    swap_w = same(WB.at[c], pair_s.at[0], pair_r.at[0], sibling)
    swap_f = same(F.at[c], pair_s.at[1], pair_r.at[1], sibling)
    swap_t = same(T.at[c], pair_s.at[2], pair_r.at[2], sibling)
    start([swap_w, swap_f])
    arrive([swap_w])
    both = jnp.concatenate([WB[0].astype(F32), WB[1].astype(F32)], axis=1)
    mine = jnp.where(c == 0, both[:, :, : 2 * HEAD], both[:, :, 2 * HEAD :]).astype(BF16)
    for h in range(2):
        cut = slice(h * HEAD, (h + 1) * HEAD)
        W[h, x, z, y] = jnp.concatenate([mine[0, :, cut], mine[1, :, cut]], axis=1)

    def four(r):
        return pl.ds(lax.rem(quad + r, 4) * 4, 4)

    def half(r, side):
        return pl.ds(lax.rem(quad + r, 4) * 4 + 2 * side, 2)

    z0 = [same(W.at[:, x, z, y], z_s.at[d], z_r.at[d], in_quad(d)) for d in range(1, 4)]
    z_up = same(W.at[:, x, four(0), y], z_s.at[4], z_r.at[4], at_z(4))
    z_down = same(W.at[:, x, four(0), y], z_s.at[5], z_r.at[5], at_z(12))
    z_far = [
        same(W.at[:, x, half(1, 0), y], z_s.at[6], z_r.at[6], at_z(12)),
        same(W.at[:, x, half(3, 1), y], z_s.at[7], z_r.at[7], at_z(4)),
    ]
    k0 = [same(KG.at[x, z], k_s.at[d], k_r.at[d], in_quad(d)) for d in range(1, 4)]
    k_up = same(KG.at[x, four(0)], k_s.at[4], k_r.at[4], at_z(4))
    k_down = same(KG.at[x, four(0)], k_s.at[5], k_r.at[5], at_z(12))
    k_far = same(KG.at[x, four(1)], k_s.at[6], k_r.at[6], at_z(12))
    k_x = [same(KG.at[x], k_s.at[7 + i], k_r.at[7 + i], at_x(d)) for i, d in enumerate((1, 3))]

    def two(r):
        a, b = W.at[0, x, four(r), y], W.at[1, x, four(r), y]
        return [same(a, two_s.at[r, 0, d], two_r.at[r, 0, d], at_y(d)) for d in (1, 3, 2)] + [
            same(b, two_s.at[r, 1, d], two_r.at[r, 1, d], at_x(d)) for d in (1, 3, 2)
        ]

    def three(r):
        a, b = W.at[0, x, four(r)], W.at[1, :, four(r), y]
        return [same(a, three_s.at[r, 0, d], three_r.at[r, 0, d], at_x(d)) for d in (1, 3)] + [
            same(b, three_s.at[r, 1, d], three_r.at[r, 1, d], at_y(d)) for d in (1, 3)
        ]

    def far(r):
        to = 1 if r in (0, 3) else 3
        a = W.at[0, lax.rem(x + 4 - to, NX), four(r)]
        b = W.at[1, :, four(r), lax.rem(y + 4 - to, NY)]
        return [
            same(a, three_s.at[r, 0, 2], three_r.at[r, 0, 2], at_x(to)),
            same(b, three_s.at[r, 1, 2], three_r.at[r, 1, 2], at_y(to)),
        ]

    depth = 4 * NY * 16

    def project(h, part, r):
        q = lax.rem(quad + r, 4)
        cols = pl.ds(pl.multiple_of((part * 4 + q) * depth, depth), depth)
        rows = T[:, :, cols].reshape(2 * HEAD, depth)
        acc[h] += jnp.dot(
            rows, W[h, part, four(r)].reshape(depth, 2 * HEAD), preferred_element_type=F32
        )

    def near_a(r):
        def one(i, carry):
            project(0, lax.rem(x + 3 + i, NX), r)
            return carry

        lax.fori_loop(0, 3, one, 0)

    def rest(r):
        project(0, lax.rem(x + 2, NX), r)

        def one(i, carry):
            project(1, i, r)
            return carry

        lax.fori_loop(0, NX, one, 0)

    start(z0)
    loads[3].wait()
    start([swap_t])
    arrive([swap_f])
    column, row, last = [], [], []
    for s in range(2):
        a, b, l = segments(F[s])
        column.append(a)
        row.append(b)
        last.append(l)
    keeps = [jnp.broadcast_to(jnp.where(l > 0, 0.0, 1.0), (4, HEAD)) for l in last]
    KG[x, z] = jnp.concatenate(keeps, axis=0)
    arrive(z0)
    start([z_up, z_down])
    start(two(0))
    start(k0)
    acc[...] = jnp.zeros_like(acc)
    arrive(k0)
    start([k_up, k_down])
    arrive(two(0))
    start(three(0))
    arrive([z_up])
    start([z_far[1]])
    start(two(3))
    arrive([z_down])
    start([z_far[0]])
    start(two(1))
    arrive([k_up, k_down])
    start([k_far])
    arrive(two(3))
    start(three(3))
    arrive(three(0))
    start(far(0))
    arrive(two(1))
    start(three(1))
    arrive(z_far)
    start(two(2))
    arrive([k_far])
    start(k_x)
    arrive([swap_t])
    near_a(0)
    arrive(three(3))
    start(far(3))
    near_a(3)
    arrive(two(2))
    start(three(2))
    arrive(three(1))
    start(far(1))
    arrive(far(0))
    rest(0)
    near_a(1)
    arrive(far(3))
    rest(3)
    arrive(three(2))
    start(far(2))
    near_a(2)
    arrive(far(1))
    rest(1)
    arrive(k_x)
    arrive(far(2))
    rest(2)

    place = lax.rem(z + NZ // 2, GROUP)
    base = lax.rem(x + NX - jnp.where(place < GROUP // 2, 0, 1), NX)

    def member_x(p):
        return lax.rem(base + p // (GROUP // 2), NX)

    def member_z(p):
        return lax.rem(p + NZ // 2, NZ)

    def member(p, core):
        return device(member_x(p), member_z(p), y, core)

    def one_copy(d):
        p = lax.rem(place + d, GROUP)
        return send(ST.at[p], SR.at[place], s1_s.at[d], s1_r.at[d], member(p, c))

    def one_start(d, carry):
        one_copy(d).start()
        return carry

    def one_wait(d, carry):
        one_copy(d).wait()
        return carry

    for s in range(2):
        tail = (column[s] == last[s]).astype(F32)
        for h in range(2):
            part = acc[h, s * HEAD : (s + 1) * HEAD, :]
            key = phi(part[:, :HEAD]).astype(BF16)
            value = part[:, HEAD:].astype(BF16)
            KV[s, 2 * c + h, 0] = key
            KV[s, 2 * c + h, 1] = value
            masked = (key.astype(F32) * tail).astype(BF16)
            state = lax.dot_general(masked, value, (((0,), (0,)), ((), ())), preferred_element_type=F32)
            slot = (s * 2 + h) * 4
            ST[slot : slot + 4] = state.astype(BF16).reshape(4, HEAD // 4, HEAD)
    lax.fori_loop(1, GROUP, one_start, 0)
    SR[place] = ST[place]
    swap_kv = same(KV.at[other, pl.ds(2 * c, 2)], pair_s.at[3], pair_r.at[3], sibling)
    start([swap_kv])

    loads[4].wait()
    loads[5].wait()
    my_column = jnp.where(c == 0, column[0], column[1])
    my_row = jnp.where(c == 0, row[0], row[1])
    t = lax.broadcasted_iota(jnp.int32, (HEAD, HEAD), 0)
    u = lax.broadcasted_iota(jnp.int32, (HEAD, HEAD), 1)
    allowed = (u <= t) & (my_column == my_row)
    Q[...] = phi(Q[...].astype(F32)).astype(BF16)
    arrive([swap_kv])
    for h in range(4):
        query = Q[:, h * HEAD : (h + 1) * HEAD]
        key, value = KV[c, h, 0], KV[c, h, 1]
        scores = lax.dot_general(query, key, (((1,), (1,)), ((), ())), preferred_element_type=F32)
        scores = jnp.where(allowed, scores, 0.0).astype(BF16)
        MIX[h] = jnp.dot(scores, value, preferred_element_type=F32)

    lax.fori_loop(1, GROUP, one_wait, 0)
    seq = place // (GROUP // 2)

    def prefix(b, carried):
        CS[b] = carried.astype(BF16)
        tile = KG[member_x(b), member_z(b)]
        keep = jnp.where(seq == 0, tile[0:1], tile[4:5])
        return keep * carried + SR[b].astype(F32)

    lax.fori_loop(0, GROUP, prefix, jnp.zeros((HEAD // 4, HEAD), F32))

    mine_at = lax.rem(place, GROUP // 2)
    target = CR.at[2 * c + mine_at // 4, lax.rem(mine_at, 4)]
    index = c * 8 + mine_at

    def back_copy(d):
        p = lax.rem(place + d, GROUP)
        return send(CS.at[p], target, s2_s.at[d], s2_r.at[index], member(p, seq))

    def back_start(d, carry):
        back_copy(d).start()
        return carry

    def back_wait(d, carry):
        back_copy(d).wait_send()
        return carry

    own = pltpu.make_async_copy(CS.at[place], target, s2_r.at[index])

    @pl.when(seq == c)
    def _():
        own.start()

    @pl.when(seq != c)
    def _():
        back_copy(0).start()

    lax.fori_loop(1, GROUP, back_start, 0)

    def back_arrive(i, carry):
        send(CS.at[0], CR.at[i // 4, lax.rem(i, 4)], s2_s.at[0], s2_r.at[i], sibling).wait_recv()
        return carry

    for copy in started:
        copy.wait_send()
    lax.fori_loop(0, GROUP, back_arrive, 0)
    first = (my_column == 0).astype(F32)
    for h in range(4):
        query = Q[:, h * HEAD : (h + 1) * HEAD]
        state = CR[h].reshape(HEAD, HEAD)
        mixed = MIX[h] + first * jnp.dot(query, state, preferred_element_type=F32)
        scale = lax.rsqrt(jnp.mean(mixed * mixed, axis=-1, keepdims=True) + 1e-06)
        cut = slice(h * HEAD, (h + 1) * HEAD)
        out[:, cut] = (mixed * scale * G[:, cut]).astype(BF16)

    @pl.when(seq != c)
    def _():
        back_copy(0).wait_send()

    lax.fori_loop(1, GROUP, back_wait, 0)


def on_device(tokens, queries, flags, w_key, w_value, norm_gain):
    count, width = queries.shape[1:]
    dma = pltpu.SemaphoreType.DMA
    any_spec = pl.BlockSpec(memory_space=pltpu.HBM)
    vmem_spec = pl.BlockSpec(memory_space=pltpu.VMEM)
    attended = pl.pallas_call(
        kernel,
        out_shape=jax.ShapeDtypeStruct((count, width), BF16),
        in_specs=[any_spec] * 6,
        out_specs=vmem_spec,
        scratch_shapes=[
            pltpu.VMEM((2, count, tokens.shape[2]), BF16),
            pltpu.VMEM((count, width), BF16),
            pltpu.VMEM((2, 1, count), jnp.int32),
            pltpu.VMEM((1, width), F32),
            pltpu.VMEM((2, 2, 8, width), BF16),
            pltpu.VMEM((2, NX, NZ, NY, 16, 2 * HEAD), BF16),
            pltpu.VMEM((2, 2 * count, 2 * HEAD), F32),
            pltpu.VMEM((2, 4, 2, count, HEAD), BF16),
            pltpu.VMEM((NX, NZ, 8, HEAD), F32),
            pltpu.VMEM((GROUP, HEAD // 4, HEAD), BF16),
            pltpu.VMEM((GROUP, HEAD // 4, HEAD), BF16),
            pltpu.VMEM((GROUP, HEAD // 4, HEAD), BF16),
            pltpu.VMEM((4, 4, HEAD // 4, HEAD), BF16),
            pltpu.VMEM((4, count, HEAD), F32),
            dma((6,)),
            dma((4,)),
            dma((4,)),
            dma((8,)),
            dma((8,)),
            dma((9,)),
            dma((9,)),
            dma((4, 2, 4)),
            dma((4, 2, 4)),
            dma((4, 2, 4)),
            dma((4, 2, 4)),
            dma((GROUP,)),
            dma((GROUP,)),
            dma((GROUP,)),
            dma((GROUP,)),
        ],
        compiler_params=pltpu.CompilerParams(
            collective_id=0, has_side_effects=True, vmem_limit_bytes=62 << 20
        ),
        name="attention",
    )(tokens[0], queries[0], flags, w_key, w_value, norm_gain.reshape(1, width))
    return attended.reshape(1, count, width)


def solution(mesh):
    in_specs = (
        P("fsdp", "ctx", None),
        P("fsdp", "ctx", None),
        P("fsdp", "ctx"),
        P(("ctx", "fsdp"), None),
        P(("ctx", "fsdp"), None),
        P(),
    )
    out_specs = P("fsdp", "ctx", None)
    return jax.shard_map(
        on_device, mesh=mesh, in_specs=in_specs, out_specs=out_specs, check_vma=False
    )
```

time: 97.9 us -> 81.9 us (0.84)
  Pallas kernels: 92 us -> 80.2 us
  local copies, waits for them, and re-layouts: 4.86 us -> 1.57 us
    pallas_call x1, Pallas kernels: 92 us -> 80.2 us  [on_device(): pl.pallas_call(kernel, out_shape=jax.ShapeDtypeStruct((count, width), BF1...]
    unnamed x13 -> x1, local copies, waits for them, and re-layouts: 4.86 us -> 1.57 us
where the time goes in v2:
time: 81.9 us; the launch traced here: 81.8 us
  Pallas kernels  80.2 us (98%)
  local copies, waits for them, and re-layouts  1.57 us (2%)
    pallas_call x1, Pallas kernels, on_device(): pl.pallas_call(kernel, out_shape=jax.ShapeDtypeStruct((count, width), BF1...  80.2 us

profile of v2, /device:TPU:24, one launch (start us, length us, event | category | flops | bytes accessed | tf_op | source)
XLA Modules:
  0.0 81.8 jit_solution(1662854258219938574)
XLA Ops:
  0.0 80.2 %attention.1 = bf16[128,512]{1,0:T(8,128)(2,1)} custom-call(bf16[128,4096]{1,0:T(8,128)(2,1)} %bitcast.4, bf16[128,512]{1,0:T(8,128)(2,1)} %bitcast.6, s32[1,128]{1,0:T(1,128)} %flg.1, bf16[8,512]{1,0:T(8,128)(2,1)} %wk.1, bf16[8,512]{1,0:T(8,128)(2,1)} %wv.1, f32[1,512]{1,0:T(1,128)} %bitcast.7), custom_call_target="tpu_custom_call" | custom-call | tf_op jit(solution)/shard_map/attention/pallas_call | solution.py:364
  80.2 1.6 %copy.8 = bf16[1,128,512]{2,1,0:T(8,128)(2,1)} copy(bf16[1,128,512]{2,1,0:T(8,128)(2,1)} %bitcast.5) | data formatting | bytes 262144

commit v3 on v2

--- a/solution.py
+++ b/solution.py
@@ -36,8 +36,8 @@
 
 def kernel(
     tok, qry, flg, wk, wv, gain, out,
-    T, Q, F, G, WB, W, acc, KV, KG, ST, SR, CS, CR, MIX,
-    loc, pair_s, pair_r, z_s, z_r, k_s, k_r, two_s, two_r, three_s, three_r, s1_s, s1_r, s2_s, s2_r,
+    T, Q, F, G, WB, W, acc, KV, TL, KB, KR, ST, SR, CS, CR, MIX,
+    loc, pair_s, pair_r, hop_s, hop_r, z_s, z_r, k_s, k_r, two_s, two_r, three_s, three_r, s1_s, s1_r, s2_s, s2_r,
 ):
     ctx, fsdp = lax.axis_index("ctx"), lax.axis_index("fsdp")
     x, z = ctx // NZ, lax.rem(ctx, NZ)
@@ -70,16 +70,23 @@
         load.start()
 
     barrier = pltpu.get_barrier_semaphore()
-    greeted = [sibling, at_z(4), at_z(12)]
-    for d in range(1, 4):
-        greeted += [at_x(d), at_y(d), in_quad(d)]
-    for to in greeted:
+
+    def greet(to):
         pl.semaphore_signal(barrier, inc=1, device_id=to, device_id_type=MESH)
+
+    def greet_xy(d, carry):
+        greet(at_x(d))
+        greet(at_y(d))
+        greet(in_quad(d))
+        return carry
+
+    lax.fori_loop(1, 4, greet_xy, 0)
+    greet(sibling)
+    greet(at_z(4))
+    greet(at_z(12))
     for load in loads[:3]:
         load.wait()
-    pl.semaphore_wait(barrier, len(greeted))
-
-    started = []
+    pl.semaphore_wait(barrier, 12)
 
     def send(src, dst, ss, rs, to):
         return pltpu.make_async_remote_copy(
@@ -92,7 +99,6 @@
     def start(copies):
         for copy in copies:
             copy.start()
-            started.append(copy)
 
     def arrive(copies):
         for copy in copies:
@@ -112,21 +118,15 @@
     def four(r):
         return pl.ds(lax.rem(quad + r, 4) * 4, 4)
 
-    def half(r, side):
-        return pl.ds(lax.rem(quad + r, 4) * 4 + 2 * side, 2)
-
-    z0 = [same(W.at[:, x, z, y], z_s.at[d], z_r.at[d], in_quad(d)) for d in range(1, 4)]
-    z_up = same(W.at[:, x, four(0), y], z_s.at[4], z_r.at[4], at_z(4))
-    z_down = same(W.at[:, x, four(0), y], z_s.at[5], z_r.at[5], at_z(12))
-    z_far = [
-        same(W.at[:, x, half(1, 0), y], z_s.at[6], z_r.at[6], at_z(12)),
-        same(W.at[:, x, half(3, 1), y], z_s.at[7], z_r.at[7], at_z(4)),
-    ]
-    k0 = [same(KG.at[x, z], k_s.at[d], k_r.at[d], in_quad(d)) for d in range(1, 4)]
-    k_up = same(KG.at[x, four(0)], k_s.at[4], k_r.at[4], at_z(4))
-    k_down = same(KG.at[x, four(0)], k_s.at[5], k_r.at[5], at_z(12))
-    k_far = same(KG.at[x, four(1)], k_s.at[6], k_r.at[6], at_z(12))
-    k_x = [same(KG.at[x], k_s.at[7 + i], k_r.at[7 + i], at_x(d)) for i, d in enumerate((1, 3))]
+    def hop(d, ahead, k):
+        piece = W.at[:, x, lax.rem(z + ahead, NZ), y]
+        return same(piece, hop_s.at[k], hop_r.at[k], at_z(d))
+
+    hops = [hop(4, 0, 0), hop(12, 0, 1), hop(12, 4, 2)]
+
+    def share(r):
+        piece = W.at[:, x, lax.rem(z + 4 * r, NZ), y]
+        return [same(piece, z_s.at[r, d], z_r.at[r, d], in_quad(d)) for d in range(1, 4)]
 
     def two(r):
         a, b = W.at[0, x, four(r), y], W.at[1, x, four(r), y]
@@ -141,7 +141,7 @@
         ]
 
     def far(r):
-        to = 1 if r in (0, 3) else 3
+        to = jnp.where(lax.rem(r, 2) == 0, 1, 3)
         a = W.at[0, lax.rem(x + 4 - to, NX), four(r)]
         b = W.at[1, :, four(r), lax.rem(y + 4 - to, NY)]
         return [
@@ -175,7 +175,21 @@
 
         lax.fori_loop(0, NX, one, 0)
 
-    start(z0)
+    place = lax.rem(z + NZ // 2, GROUP)
+    base = lax.rem(x + NX - jnp.where(place < GROUP // 2, 0, 1), NX)
+
+    def member(p, core):
+        return device(lax.rem(base + p // (GROUP // 2), NX), lax.rem(p + NZ // 2, NZ), y, core)
+
+    def keep_copy(d):
+        return send(KB, KR.at[place], k_s.at[d], k_r.at[d], member(lax.rem(place + d, GROUP), c))
+
+    def keep_start(d, carry):
+        keep_copy(d).start()
+        return carry
+
+    start(hops[:2])
+    start(share(0))
     loads[3].wait()
     start([swap_t])
     arrive([swap_f])
@@ -186,68 +200,54 @@
         row.append(b)
         last.append(l)
     keeps = [jnp.broadcast_to(jnp.where(l > 0, 0.0, 1.0), (4, HEAD)) for l in last]
-    KG[x, z] = jnp.concatenate(keeps, axis=0)
-    arrive(z0)
-    start([z_up, z_down])
+    KB[...] = jnp.concatenate(keeps, axis=0)
+    KR[place] = KB[...]
+    acc[...] = jnp.zeros_like(acc)
+
+    arrive(share(0))
     start(two(0))
-    start(k0)
-    acc[...] = jnp.zeros_like(acc)
-    arrive(k0)
-    start([k_up, k_down])
+    arrive(hops[:2])
+    start(hops[2:])
+    start(share(1))
+    start(share(3))
     arrive(two(0))
     start(three(0))
-    arrive([z_up])
-    start([z_far[1]])
+    arrive(hops[2:])
+    start(share(2))
+    arrive(share(1))
+    start(two(1))
+    arrive(share(3))
     start(two(3))
-    arrive([z_down])
-    start([z_far[0]])
-    start(two(1))
-    arrive([k_up, k_down])
-    start([k_far])
+    arrive(three(0))
+    start(far(0))
+    arrive(share(2))
+    start(two(2))
+    arrive(two(1))
+    start(three(1))
     arrive(two(3))
     start(three(3))
-    arrive(three(0))
-    start(far(0))
-    arrive(two(1))
-    start(three(1))
-    arrive(z_far)
-    start(two(2))
-    arrive([k_far])
-    start(k_x)
     arrive([swap_t])
     near_a(0)
-    arrive(three(3))
-    start(far(3))
-    near_a(3)
+    arrive(far(0))
+    rest(0)
     arrive(two(2))
     start(three(2))
     arrive(three(1))
     start(far(1))
-    arrive(far(0))
-    rest(0)
+    arrive(three(3))
+    start(far(3))
     near_a(1)
+    near_a(3)
+    arrive(three(2))
+    start(far(2))
+    lax.fori_loop(1, GROUP, keep_start, 0)
+    arrive(far(1))
+    rest(1)
     arrive(far(3))
     rest(3)
-    arrive(three(2))
-    start(far(2))
     near_a(2)
-    arrive(far(1))
-    rest(1)
-    arrive(k_x)
     arrive(far(2))
     rest(2)
-
-    place = lax.rem(z + NZ // 2, GROUP)
-    base = lax.rem(x + NX - jnp.where(place < GROUP // 2, 0, 1), NX)
-
-    def member_x(p):
-        return lax.rem(base + p // (GROUP // 2), NX)
-
-    def member_z(p):
-        return lax.rem(p + NZ // 2, NZ)
-
-    def member(p, core):
-        return device(member_x(p), member_z(p), y, core)
 
     def one_copy(d):
         p = lax.rem(place + d, GROUP)
@@ -259,20 +259,25 @@
 
     def one_wait(d, carry):
         one_copy(d).wait()
+        keep_copy(d).wait()
         return carry
 
     for s in range(2):
-        tail = (column[s] == last[s]).astype(F32)
-        for h in range(2):
-            part = acc[h, s * HEAD : (s + 1) * HEAD, :]
-            key = phi(part[:, :HEAD]).astype(BF16)
-            value = part[:, HEAD:].astype(BF16)
-            KV[s, 2 * c + h, 0] = key
-            KV[s, 2 * c + h, 1] = value
-            masked = (key.astype(F32) * tail).astype(BF16)
-            state = lax.dot_general(masked, value, (((0,), (0,)), ((), ())), preferred_element_type=F32)
-            slot = (s * 2 + h) * 4
-            ST[slot : slot + 4] = state.astype(BF16).reshape(4, HEAD // 4, HEAD)
+        TL[s] = jnp.broadcast_to((column[s] == last[s]).astype(F32), (HEAD, HEAD))
+
+    def states(i, carry):
+        s, h = i // 2, lax.rem(i, 2)
+        part = acc[h, pl.ds(pl.multiple_of(s * HEAD, HEAD), HEAD), :]
+        key = phi(part[:, :HEAD]).astype(BF16)
+        value = part[:, HEAD:].astype(BF16)
+        KV[s, 2 * c + h, 0] = key
+        KV[s, 2 * c + h, 1] = value
+        masked = (key.astype(F32) * TL[s]).astype(BF16)
+        state = lax.dot_general(masked, value, (((0,), (0,)), ((), ())), preferred_element_type=F32)
+        ST[pl.ds(4 * i, 4)] = state.astype(BF16).reshape(4, HEAD // 4, HEAD)
+        return carry
+
+    lax.fori_loop(0, 4, states, 0)
     lax.fori_loop(1, GROUP, one_start, 0)
     SR[place] = ST[place]
     swap_kv = same(KV.at[other, pl.ds(2 * c, 2)], pair_s.at[3], pair_r.at[3], sibling)
@@ -287,19 +292,23 @@
     allowed = (u <= t) & (my_column == my_row)
     Q[...] = phi(Q[...].astype(F32)).astype(BF16)
     arrive([swap_kv])
-    for h in range(4):
-        query = Q[:, h * HEAD : (h + 1) * HEAD]
+    mask = allowed.astype(F32)
+
+    def inside(h, carry):
+        query = Q[:, pl.ds(pl.multiple_of(h * HEAD, HEAD), HEAD)]
         key, value = KV[c, h, 0], KV[c, h, 1]
         scores = lax.dot_general(query, key, (((1,), (1,)), ((), ())), preferred_element_type=F32)
-        scores = jnp.where(allowed, scores, 0.0).astype(BF16)
+        scores = (scores * mask).astype(BF16)
         MIX[h] = jnp.dot(scores, value, preferred_element_type=F32)
-
+        return carry
+
+    lax.fori_loop(0, 4, inside, 0)
     lax.fori_loop(1, GROUP, one_wait, 0)
     seq = place // (GROUP // 2)
 
     def prefix(b, carried):
         CS[b] = carried.astype(BF16)
-        tile = KG[member_x(b), member_z(b)]
+        tile = KR[b]
         keep = jnp.where(seq == 0, tile[0:1], tile[4:5])
         return keep * carried + SR[b].astype(F32)
 
@@ -337,17 +346,26 @@
         send(CS.at[0], CR.at[i // 4, lax.rem(i, 4)], s2_s.at[0], s2_r.at[i], sibling).wait_recv()
         return carry
 
-    for copy in started:
+    def drain(r, carry):
+        for copy in share(r) + two(r) + three(r) + far(r):
+            copy.wait_send()
+        return carry
+
+    lax.fori_loop(0, 4, drain, 0)
+    for copy in hops + [swap_w, swap_f, swap_t, swap_kv]:
         copy.wait_send()
     lax.fori_loop(0, GROUP, back_arrive, 0)
     first = (my_column == 0).astype(F32)
-    for h in range(4):
-        query = Q[:, h * HEAD : (h + 1) * HEAD]
+
+    def finish(h, carry):
+        cut = pl.ds(pl.multiple_of(h * HEAD, HEAD), HEAD)
         state = CR[h].reshape(HEAD, HEAD)
-        mixed = MIX[h] + first * jnp.dot(query, state, preferred_element_type=F32)
+        mixed = MIX[h] + first * jnp.dot(Q[:, cut], state, preferred_element_type=F32)
         scale = lax.rsqrt(jnp.mean(mixed * mixed, axis=-1, keepdims=True) + 1e-06)
-        cut = slice(h * HEAD, (h + 1) * HEAD)
         out[:, cut] = (mixed * scale * G[:, cut]).astype(BF16)
+        return carry
+
+    lax.fori_loop(0, 4, finish, 0)
 
     @pl.when(seq != c)
     def _():
@@ -375,7 +393,9 @@
             pltpu.VMEM((2, NX, NZ, NY, 16, 2 * HEAD), BF16),
             pltpu.VMEM((2, 2 * count, 2 * HEAD), F32),
             pltpu.VMEM((2, 4, 2, count, HEAD), BF16),
-            pltpu.VMEM((NX, NZ, 8, HEAD), F32),
+            pltpu.VMEM((2, HEAD, HEAD), F32),
+            pltpu.VMEM((8, HEAD), F32),
+            pltpu.VMEM((GROUP, 8, HEAD), F32),
             pltpu.VMEM((GROUP, HEAD // 4, HEAD), BF16),
             pltpu.VMEM((GROUP, HEAD // 4, HEAD), BF16),
             pltpu.VMEM((GROUP, HEAD // 4, HEAD), BF16),
@@ -384,10 +404,12 @@
             dma((6,)),
             dma((4,)),
             dma((4,)),
-            dma((8,)),
-            dma((8,)),
-            dma((9,)),
-            dma((9,)),
+            dma((3,)),
+            dma((3,)),
+            dma((4, 4)),
+            dma((4, 4)),
+            dma((GROUP,)),
+            dma((GROUP,)),
             dma((4, 2, 4)),
             dma((4, 2, 4)),
             dma((4, 2, 4)),

time: 81.9 us -> 76.1 us (0.929); the launches traced: 81.8 us -> 75 us
  Pallas kernels: 80.2 us -> 73.4 us
    pallas_call x1, Pallas kernels: 80.2 us -> 73.4 us  [on_device(): pl.pallas_call(kernel, out_shape=jax.ShapeDtypeStruct((count, width), BF1...]
where the time goes in v3:
time: 76.1 us; the launch traced here: 75 us
  Pallas kernels  73.4 us (96%)
  local copies, waits for them, and re-layouts  1.57 us (2%)
    pallas_call x1, Pallas kernels, on_device(): pl.pallas_call(kernel, out_shape=jax.ShapeDtypeStruct((count, width), BF1...  73.4 us
    unnamed x1, local copies, waits for them, and re-layouts  1.57 us

profile of v3, /device:TPU:24, one launch (start us, length us, event | category | flops | bytes accessed | tf_op | source)
XLA Modules:
  0.0 75.0 jit_solution(15398539019555680189)
XLA Ops:
  0.0 73.4 %attention.1 = bf16[128,512]{1,0:T(8,128)(2,1)} custom-call(bf16[128,4096]{1,0:T(8,128)(2,1)} %bitcast.4, bf16[128,512]{1,0:T(8,128)(2,1)} %bitcast.6, s32[1,128]{1,0:T(1,128)} %flg.1, bf16[8,512]{1,0:T(8,128)(2,1)} %wk.1, bf16[8,512]{1,0:T(8,128)(2,1)} %wv.1, f32[1,512]{1,0:T(1,128)} %bitcast.7), custom_call_target="tpu_custom_call" | custom-call | tf_op jit(solution)/shard_map/attention/pallas_call | solution.py:382
  73.4 1.6 %copy.8 = bf16[1,128,512]{2,1,0:T(8,128)(2,1)} copy(bf16[1,128,512]{2,1,0:T(8,128)(2,1)} %bitcast.5) | data formatting | bytes 262144

commit v4 on v3

--- a/solution.py
+++ b/solution.py
@@ -36,7 +36,7 @@
 
 def kernel(
     tok, qry, flg, wk, wv, gain, out,
-    T, Q, F, G, WB, W, acc, KV, TL, KB, KR, ST, SR, CS, CR, MIX,
+    T, Q, F, G, WB, W, acc, KV, TL, KG, ST, SR, CS, CR, MIX,
     loc, pair_s, pair_r, hop_s, hop_r, z_s, z_r, k_s, k_r, two_s, two_r, three_s, three_r, s1_s, s1_r, s2_s, s2_r,
 ):
     ctx, fsdp = lax.axis_index("ctx"), lax.axis_index("fsdp")
@@ -178,15 +178,26 @@
     place = lax.rem(z + NZ // 2, GROUP)
     base = lax.rem(x + NX - jnp.where(place < GROUP // 2, 0, 1), NX)
 
+    def member_x(p):
+        return lax.rem(base + p // (GROUP // 2), NX)
+
+    def member_z(p):
+        return lax.rem(p + NZ // 2, NZ)
+
     def member(p, core):
-        return device(lax.rem(base + p // (GROUP // 2), NX), lax.rem(p + NZ // 2, NZ), y, core)
-
-    def keep_copy(d):
-        return send(KB, KR.at[place], k_s.at[d], k_r.at[d], member(lax.rem(place + d, GROUP), c))
-
-    def keep_start(d, carry):
-        keep_copy(d).start()
-        return carry
+        return device(member_x(p), member_z(p), y, core)
+
+    def keep_four(r):
+        return KG.at[x, four(r)]
+
+    keep_in = [same(KG.at[x, z], k_s.at[d], k_r.at[d], in_quad(d)) for d in range(1, 4)]
+    keep_z = [
+        same(keep_four(0), k_s.at[4], k_r.at[4], at_z(4)),
+        same(keep_four(0), k_s.at[5], k_r.at[5], at_z(12)),
+    ]
+    keep_far = [same(keep_four(1), k_s.at[6], k_r.at[6], at_z(12))]
+    keep_x = [same(KG.at[x], k_s.at[6 + d], k_r.at[6 + d], at_x(d)) for d in (1, 3)]
+    keep_all = keep_in + keep_z + keep_far + keep_x
 
     start(hops[:2])
     start(share(0))
@@ -200,8 +211,8 @@
         row.append(b)
         last.append(l)
     keeps = [jnp.broadcast_to(jnp.where(l > 0, 0.0, 1.0), (4, HEAD)) for l in last]
-    KB[...] = jnp.concatenate(keeps, axis=0)
-    KR[place] = KB[...]
+    KG[x, z] = jnp.concatenate(keeps, axis=0)
+    start(keep_in)
     acc[...] = jnp.zeros_like(acc)
 
     arrive(share(0))
@@ -212,6 +223,8 @@
     start(share(3))
     arrive(two(0))
     start(three(0))
+    arrive(keep_in)
+    start(keep_z)
     arrive(hops[2:])
     start(share(2))
     arrive(share(1))
@@ -222,6 +235,8 @@
     start(far(0))
     arrive(share(2))
     start(two(2))
+    arrive(keep_z)
+    start(keep_far)
     arrive(two(1))
     start(three(1))
     arrive(two(3))
@@ -236,11 +251,12 @@
     start(far(1))
     arrive(three(3))
     start(far(3))
+    arrive(keep_far)
+    start(keep_x)
     near_a(1)
     near_a(3)
     arrive(three(2))
     start(far(2))
-    lax.fori_loop(1, GROUP, keep_start, 0)
     arrive(far(1))
     rest(1)
     arrive(far(3))
@@ -249,17 +265,20 @@
     arrive(far(2))
     rest(2)
 
+    def distant(i):
+        step = (i + 1) // 2
+        return jnp.where(lax.rem(i, 2) == 1, GROUP // 2 - step, GROUP // 2 + step)
+
     def one_copy(d):
         p = lax.rem(place + d, GROUP)
         return send(ST.at[p], SR.at[place], s1_s.at[d], s1_r.at[d], member(p, c))
 
     def one_start(d, carry):
-        one_copy(d).start()
+        one_copy(distant(d)).start()
         return carry
 
     def one_wait(d, carry):
         one_copy(d).wait()
-        keep_copy(d).wait()
         return carry
 
     for s in range(2):
@@ -277,8 +296,8 @@
         ST[pl.ds(4 * i, 4)] = state.astype(BF16).reshape(4, HEAD // 4, HEAD)
         return carry
 
-    lax.fori_loop(0, 4, states, 0)
-    lax.fori_loop(1, GROUP, one_start, 0)
+    lax.fori_loop(0, 4, states, 0, unroll=True)
+    lax.fori_loop(0, GROUP - 1, one_start, 0)
     SR[place] = ST[place]
     swap_kv = same(KV.at[other, pl.ds(2 * c, 2)], pair_s.at[3], pair_r.at[3], sibling)
     start([swap_kv])
@@ -302,13 +321,14 @@
         MIX[h] = jnp.dot(scores, value, preferred_element_type=F32)
         return carry
 
-    lax.fori_loop(0, 4, inside, 0)
+    lax.fori_loop(0, 4, inside, 0, unroll=True)
     lax.fori_loop(1, GROUP, one_wait, 0)
+    arrive(keep_x)
     seq = place // (GROUP // 2)
 
     def prefix(b, carried):
         CS[b] = carried.astype(BF16)
-        tile = KR[b]
+        tile = KG[member_x(b), member_z(b)]
         keep = jnp.where(seq == 0, tile[0:1], tile[4:5])
         return keep * carried + SR[b].astype(F32)
 
@@ -323,7 +343,7 @@
         return send(CS.at[p], target, s2_s.at[d], s2_r.at[index], member(p, seq))
 
     def back_start(d, carry):
-        back_copy(d).start()
+        back_copy(distant(d)).start()
         return carry
 
     def back_wait(d, carry):
@@ -331,6 +351,8 @@
         return carry
 
     own = pltpu.make_async_copy(CS.at[place], target, s2_r.at[index])
+
+    lax.fori_loop(0, GROUP - 1, back_start, 0)
 
     @pl.when(seq == c)
     def _():
@@ -340,8 +362,6 @@
     def _():
         back_copy(0).start()
 
-    lax.fori_loop(1, GROUP, back_start, 0)
-
     def back_arrive(i, carry):
         send(CS.at[0], CR.at[i // 4, lax.rem(i, 4)], s2_s.at[0], s2_r.at[i], sibling).wait_recv()
         return carry
@@ -352,7 +372,7 @@
         return carry
 
     lax.fori_loop(0, 4, drain, 0)
-    for copy in hops + [swap_w, swap_f, swap_t, swap_kv]:
+    for copy in hops + keep_all + [swap_w, swap_f, swap_t, swap_kv]:
         copy.wait_send()
     lax.fori_loop(0, GROUP, back_arrive, 0)
     first = (my_column == 0).astype(F32)
@@ -365,7 +385,7 @@
         out[:, cut] = (mixed * scale * G[:, cut]).astype(BF16)
         return carry
 
-    lax.fori_loop(0, 4, finish, 0)
+    lax.fori_loop(0, 4, finish, 0, unroll=True)
 
     @pl.when(seq != c)
     def _():
@@ -394,8 +414,7 @@
             pltpu.VMEM((2, 2 * count, 2 * HEAD), F32),
             pltpu.VMEM((2, 4, 2, count, HEAD), BF16),
             pltpu.VMEM((2, HEAD, HEAD), F32),
-            pltpu.VMEM((8, HEAD), F32),
-            pltpu.VMEM((GROUP, 8, HEAD), F32),
+            pltpu.VMEM((NX, NZ, 8, HEAD), F32),
             pltpu.VMEM((GROUP, HEAD // 4, HEAD), BF16),
             pltpu.VMEM((GROUP, HEAD // 4, HEAD), BF16),
             pltpu.VMEM((GROUP, HEAD // 4, HEAD), BF16),
@@ -408,8 +427,8 @@
             dma((3,)),
             dma((4, 4)),
             dma((4, 4)),
-            dma((GROUP,)),
-            dma((GROUP,)),
+            dma((10,)),
+            dma((10,)),
             dma((4, 2, 4)),
             dma((4, 2, 4)),
             dma((4, 2, 4)),

time: 76.1 us -> 74.5 us (0.979)
  the two profiles are of different devices: /device:TPU:24 before, /device:TPU:1 now
where the time goes in v4:
time: 74.5 us; the launch traced here: 74.3 us
  Pallas kernels  72.7 us (98%)
  local copies, waits for them, and re-layouts  1.57 us (2%)
    pallas_call x1, Pallas kernels, on_device(): pl.pallas_call(kernel, out_shape=jax.ShapeDtypeStruct((count, width), BF1...  72.7 us
    unnamed x1, local copies, waits for them, and re-layouts  1.57 us

profile of v4, /device:TPU:1, one launch (start us, length us, event | category | flops | bytes accessed | tf_op | source)
XLA Modules:
  0.0 74.3 jit_solution(1123181879893993399)
XLA Ops:
  0.0 72.7 %attention.1 = bf16[128,512]{1,0:T(8,128)(2,1)} custom-call(bf16[128,4096]{1,0:T(8,128)(2,1)} %bitcast.4, bf16[128,512]{1,0:T(8,128)(2,1)} %bitcast.6, s32[1,128]{1,0:T(1,128)} %flg.1, bf16[8,512]{1,0:T(8,128)(2,1)} %wk.1, bf16[8,512]{1,0:T(8,128)(2,1)} %wv.1, f32[1,512]{1,0:T(1,128)} %bitcast.7), custom_call_target="tpu_custom_call" | custom-call | tf_op jit(solution)/shard_map/attention/pallas_call | solution.py:402
  72.8 1.6 %copy.8 = bf16[1,128,512]{2,1,0:T(8,128)(2,1)} copy(bf16[1,128,512]{2,1,0:T(8,128)(2,1)} %bitcast.5) | data formatting | bytes 262144

commit v5 on v4

--- a/solution.py
+++ b/solution.py
@@ -66,8 +66,6 @@
         pltpu.make_async_copy(qry, Q, loc.at[4]),
         pltpu.make_async_copy(gain, G, loc.at[5]),
     ]
-    for load in loads:
-        load.start()
 
     barrier = pltpu.get_barrier_semaphore()
 
@@ -80,10 +78,12 @@
         greet(in_quad(d))
         return carry
 
-    lax.fori_loop(1, 4, greet_xy, 0)
-    greet(sibling)
     greet(at_z(4))
     greet(at_z(12))
+    lax.fori_loop(1, 4, greet_xy, 0, unroll=True)
+    greet(sibling)
+    for load in loads:
+        load.start()
     for load in loads[:3]:
         load.wait()
     pl.semaphore_wait(barrier, 12)
@@ -141,13 +141,17 @@
         ]
 
     def far(r):
-        to = jnp.where(lax.rem(r, 2) == 0, 1, 3)
-        a = W.at[0, lax.rem(x + 4 - to, NX), four(r)]
-        b = W.at[1, :, four(r), lax.rem(y + 4 - to, NY)]
-        return [
-            same(a, three_s.at[r, 0, 2], three_r.at[r, 0, 2], at_x(to)),
-            same(b, three_s.at[r, 1, 2], three_r.at[r, 1, 2], at_y(to)),
-        ]
+        copies = []
+        for side, (to, back) in enumerate(((1, 3), (3, 1))):
+            part = pl.ds(lax.rem(quad + r, 4) * 4 + 2 * side, 2)
+            a = W.at[0, lax.rem(x + back, NX), part]
+            b = W.at[1, :, part, lax.rem(y + back, NY)]
+            k = 2 - 2 * side
+            copies += [
+                same(a, three_s.at[r, 0, k], three_r.at[r, 0, k], at_x(to)),
+                same(b, three_s.at[r, 1, k], three_r.at[r, 1, k], at_y(to)),
+            ]
+        return copies
 
     depth = 4 * NY * 16
 
@@ -160,20 +164,25 @@
         )
 
     def near_a(r):
-        def one(i, carry):
-            project(0, lax.rem(x + 3 + i, NX), r)
-            return carry
-
-        lax.fori_loop(0, 3, one, 0)
+        q = lax.rem(quad + r, 4)
+        parts = [lax.rem(x + 3 + i, NX) for i in range(3)]
+        rows = jnp.concatenate(
+            [T[:, :, pl.ds(pl.multiple_of((i * 4 + q) * depth, depth), depth)] for i in parts], axis=2
+        )
+        sides = jnp.concatenate([W[0, i, four(r)].reshape(depth, 2 * HEAD) for i in parts], axis=0)
+        acc[0] += jnp.dot(rows.reshape(2 * HEAD, 3 * depth), sides, preferred_element_type=F32)
 
     def rest(r):
         project(0, lax.rem(x + 2, NX), r)
-
-        def one(i, carry):
-            project(1, i, r)
-            return carry
-
-        lax.fori_loop(0, NX, one, 0)
+        q = lax.rem(quad + r, 4)
+        rows = jnp.concatenate(
+            [T[:, :, pl.ds(pl.multiple_of((i * 4 + q) * depth, depth), depth)] for i in range(NX)], axis=2
+        )
+        acc[1] += jnp.dot(
+            rows.reshape(2 * HEAD, NX * depth),
+            W[1, :, four(r)].reshape(NX * depth, 2 * HEAD),
+            preferred_element_type=F32,
+        )
 
     place = lax.rem(z + NZ // 2, GROUP)
     base = lax.rem(x + NX - jnp.where(place < GROUP // 2, 0, 1), NX)
@@ -253,10 +262,13 @@
     start(far(3))
     arrive(keep_far)
     start(keep_x)
+    near, ahead = three(2), far(2)
+    arrive([near[0], near[2]])
+    start(ahead[:2])
+    arrive([near[1], near[3]])
+    start(ahead[2:])
     near_a(1)
     near_a(3)
-    arrive(three(2))
-    start(far(2))
     arrive(far(1))
     rest(1)
     arrive(far(3))
@@ -297,7 +309,7 @@
         return carry
 
     lax.fori_loop(0, 4, states, 0, unroll=True)
-    lax.fori_loop(0, GROUP - 1, one_start, 0)
+    lax.fori_loop(0, GROUP - 1, one_start, 0, unroll=True)
     SR[place] = ST[place]
     swap_kv = same(KV.at[other, pl.ds(2 * c, 2)], pair_s.at[3], pair_r.at[3], sibling)
     start([swap_kv])
@@ -352,7 +364,7 @@
 
     own = pltpu.make_async_copy(CS.at[place], target, s2_r.at[index])
 
-    lax.fori_loop(0, GROUP - 1, back_start, 0)
+    lax.fori_loop(0, GROUP - 1, back_start, 0, unroll=True)
 
     @pl.when(seq == c)
     def _():

time: 74.5 us -> 73 us (0.980)
  the two profiles are of different devices: /device:TPU:1 before, /device:TPU:24 now
where the time goes in v5:
time: 73 us; the launch traced here: 72.8 us
  Pallas kernels  71.2 us (98%)
  local copies, waits for them, and re-layouts  1.57 us (2%)
    pallas_call x1, Pallas kernels, on_device(): pl.pallas_call(kernel, out_shape=jax.ShapeDtypeStruct((count, width), BF1...  71.2 us
    unnamed x1, local copies, waits for them, and re-layouts  1.57 us

profile of v5, /device:TPU:24, one launch (start us, length us, event | category | flops | bytes accessed | tf_op | source)
XLA Modules:
  0.0 72.8 jit_solution(3300015589353044968)
XLA Ops:
  0.0 71.2 %attention.1 = bf16[128,512]{1,0:T(8,128)(2,1)} custom-call(bf16[128,4096]{1,0:T(8,128)(2,1)} %bitcast.4, bf16[128,512]{1,0:T(8,128)(2,1)} %bitcast.6, s32[1,128]{1,0:T(1,128)} %flg.1, bf16[8,512]{1,0:T(8,128)(2,1)} %wk.1, bf16[8,512]{1,0:T(8,128)(2,1)} %wv.1, f32[1,512]{1,0:T(1,128)} %bitcast.7), custom_call_target="tpu_custom_call" | custom-call | tf_op jit(solution)/shard_map/attention/pallas_call | solution.py:414
  71.3 1.6 %copy.8 = bf16[1,128,512]{2,1,0:T(8,128)(2,1)} copy(bf16[1,128,512]{2,1,0:T(8,128)(2,1)} %bitcast.5) | data formatting | bytes 262144

commit v6 on v5

--- a/solution.py
+++ b/solution.py
@@ -226,9 +226,10 @@
 
     arrive(share(0))
     start(two(0))
-    arrive(hops[:2])
+    arrive([hops[1]])
     start(hops[2:])
     start(share(1))
+    arrive([hops[0]])
     start(share(3))
     arrive(two(0))
     start(three(0))

time: 73 us -> 72.4 us (level)
  no operation moved by 1% of the time
where the time goes in v6:
time: 72.4 us; the launch traced here: 72.2 us
  Pallas kernels  70.6 us (98%)
  local copies, waits for them, and re-layouts  1.57 us (2%)
    pallas_call x1, Pallas kernels, on_device(): pl.pallas_call(kernel, out_shape=jax.ShapeDtypeStruct((count, width), BF1...  70.6 us
    unnamed x1, local copies, waits for them, and re-layouts  1.57 us

profile of v6, /device:TPU:24, one launch (start us, length us, event | category | flops | bytes accessed | tf_op | source)
XLA Modules:
  0.0 72.2 jit_solution(16646139948613109838)
XLA Ops:
  0.0 70.6 %attention.1 = bf16[128,512]{1,0:T(8,128)(2,1)} custom-call(bf16[128,4096]{1,0:T(8,128)(2,1)} %bitcast.4, bf16[128,512]{1,0:T(8,128)(2,1)} %bitcast.6, s32[1,128]{1,0:T(1,128)} %flg.1, bf16[8,512]{1,0:T(8,128)(2,1)} %wk.1, bf16[8,512]{1,0:T(8,128)(2,1)} %wv.1, f32[1,512]{1,0:T(1,128)} %bitcast.7), custom_call_target="tpu_custom_call" | custom-call | tf_op jit(solution)/shard_map/attention/pallas_call | solution.py:415
  70.6 1.6 %copy.8 = bf16[1,128,512]{2,1,0:T(8,128)(2,1)} copy(bf16[1,128,512]{2,1,0:T(8,128)(2,1)} %bitcast.5) | data formatting | bytes 262144

commit v7 on v6

--- a/solution.py
+++ b/solution.py
@@ -241,8 +241,11 @@
     start(two(1))
     arrive(share(3))
     start(two(3))
-    arrive(three(0))
-    start(far(0))
+    near, ahead = three(0), far(0)
+    arrive([near[0], near[2]])
+    start(ahead[:2])
+    arrive([near[1], near[3]])
+    start(ahead[2:])
     arrive(share(2))
     start(two(2))
     arrive(keep_z)
@@ -257,10 +260,16 @@
     rest(0)
     arrive(two(2))
     start(three(2))
-    arrive(three(1))
-    start(far(1))
-    arrive(three(3))
-    start(far(3))
+    near, ahead = three(1), far(1)
+    arrive([near[0], near[2]])
+    start(ahead[:2])
+    arrive([near[1], near[3]])
+    start(ahead[2:])
+    near, ahead = three(3), far(3)
+    arrive([near[0], near[2]])
+    start(ahead[:2])
+    arrive([near[1], near[3]])
+    start(ahead[2:])
     arrive(keep_far)
     start(keep_x)
     near, ahead = three(2), far(2)
@@ -345,7 +354,7 @@
         keep = jnp.where(seq == 0, tile[0:1], tile[4:5])
         return keep * carried + SR[b].astype(F32)
 
-    lax.fori_loop(0, GROUP, prefix, jnp.zeros((HEAD // 4, HEAD), F32))
+    lax.fori_loop(0, GROUP, prefix, jnp.zeros((HEAD // 4, HEAD), F32), unroll=True)
 
     mine_at = lax.rem(place, GROUP // 2)
     target = CR.at[2 * c + mine_at // 4, lax.rem(mine_at, 4)]

time: 72.4 us -> 72.2 us (level)
  Pallas kernels: 70.6 us -> 69.8 us
    pallas_call x1, Pallas kernels: 70.6 us -> 69.8 us  [on_device(): pl.pallas_call(kernel, out_shape=jax.ShapeDtypeStruct((count, width), BF1...]
where the time goes in v7:
time: 72.2 us; the launch traced here: 71.3 us
  Pallas kernels  69.8 us (97%)
  local copies, waits for them, and re-layouts  1.57 us (2%)
    pallas_call x1, Pallas kernels, on_device(): pl.pallas_call(kernel, out_shape=jax.ShapeDtypeStruct((count, width), BF1...  69.8 us
    unnamed x1, local copies, waits for them, and re-layouts  1.57 us

profile of v7, /device:TPU:24, one launch (start us, length us, event | category | flops | bytes accessed | tf_op | source)
XLA Modules:
  0.0 71.3 jit_solution(13822398963105667545)
XLA Ops:
  0.0 69.8 %attention.1 = bf16[128,512]{1,0:T(8,128)(2,1)} custom-call(bf16[128,4096]{1,0:T(8,128)(2,1)} %bitcast.4, bf16[128,512]{1,0:T(8,128)(2,1)} %bitcast.6, s32[1,128]{1,0:T(1,128)} %flg.1, bf16[8,512]{1,0:T(8,128)(2,1)} %wk.1, bf16[8,512]{1,0:T(8,128)(2,1)} %wv.1, f32[1,512]{1,0:T(1,128)} %bitcast.7), custom_call_target="tpu_custom_call" | custom-call | tf_op jit(solution)/shard_map/attention/pallas_call | solution.py:424
  69.8 1.6 %copy.8 = bf16[1,128,512]{2,1,0:T(8,128)(2,1)} copy(bf16[1,128,512]{2,1,0:T(8,128)(2,1)} %bitcast.5) | data formatting | bytes 262144

commit v8 on v7

--- a/solution.py
+++ b/solution.py
@@ -231,8 +231,11 @@
     start(share(1))
     arrive([hops[0]])
     start(share(3))
-    arrive(two(0))
-    start(three(0))
+    earlier, later = two(0), three(0)
+    arrive(earlier[:3])
+    start(later[:2])
+    arrive(earlier[3:])
+    start(later[2:])
     arrive(keep_in)
     start(keep_z)
     arrive(hops[2:])
@@ -250,16 +253,25 @@
     start(two(2))
     arrive(keep_z)
     start(keep_far)
-    arrive(two(1))
-    start(three(1))
-    arrive(two(3))
-    start(three(3))
+    earlier, later = two(1), three(1)
+    arrive(earlier[:3])
+    start(later[:2])
+    arrive(earlier[3:])
+    start(later[2:])
+    earlier, later = two(3), three(3)
+    arrive(earlier[:3])
+    start(later[:2])
+    arrive(earlier[3:])
+    start(later[2:])
     arrive([swap_t])
     near_a(0)
     arrive(far(0))
     rest(0)
-    arrive(two(2))
-    start(three(2))
+    earlier, later = two(2), three(2)
+    arrive(earlier[:3])
+    start(later[:2])
+    arrive(earlier[3:])
+    start(later[2:])
     near, ahead = three(1), far(1)
     arrive([near[0], near[2]])
     start(ahead[:2])

time: 72.2 us -> 72.1 us (level)
  no operation moved by 1% of the time
where the time goes in v8:
time: 72.1 us; the launch traced here: 71.3 us
  Pallas kernels  69.8 us (97%)
  local copies, waits for them, and re-layouts  1.57 us (2%)
    pallas_call x1, Pallas kernels, on_device(): pl.pallas_call(kernel, out_shape=jax.ShapeDtypeStruct((count, width), BF1...  69.8 us
    unnamed x1, local copies, waits for them, and re-layouts  1.57 us

profile of v8, /device:TPU:24, one launch (start us, length us, event | category | flops | bytes accessed | tf_op | source)
XLA Modules:
  0.0 71.3 jit_solution(18090747020259492080)
XLA Ops:
  0.0 69.8 %attention.1 = bf16[128,512]{1,0:T(8,128)(2,1)} custom-call(bf16[128,4096]{1,0:T(8,128)(2,1)} %bitcast.4, bf16[128,512]{1,0:T(8,128)(2,1)} %bitcast.6, s32[1,128]{1,0:T(1,128)} %flg.1, bf16[8,512]{1,0:T(8,128)(2,1)} %wk.1, bf16[8,512]{1,0:T(8,128)(2,1)} %wv.1, f32[1,512]{1,0:T(1,128)} %bitcast.7), custom_call_target="tpu_custom_call" | custom-call | tf_op jit(solution)/shard_map/attention/pallas_call | solution.py:436
  69.8 1.6 %copy.8 = bf16[1,128,512]{2,1,0:T(8,128)(2,1)} copy(bf16[1,128,512]{2,1,0:T(8,128)(2,1)} %bitcast.5) | data formatting | bytes 262144
